TPU v7x, 32 devices: a whole 2x2x4 slice. The times are simulated.
32 devices in a mesh: row: 4 (over y, x), col: 8 (over z, core).
Axes of the slice: x: 2, y: 2, z: 4, core: 2. Of those that a mesh axis runs over, the one named last changes fastest.
Arguments:
- weights: bfloat16 [3072, 3072], P('col', 'row'), may hold values from -0.109375 to 0.109375
- weight_flags: int32 [24, 24], P('col', 'row'), may hold values from 0 to 1, as said below
- hamiltonian: bfloat16 [3072, 4096], P('row', 'col'), may hold values from -6 to 6
- ham_flags: int32 [24, 32], P('row', 'col'), may hold values from 0 to 1, as said below
Outputs:
- coupling: bfloat16 [3072, 4096], P('row', 'col')
Inputs may be any that keep to these rules, and one draw needn't show every extreme that they name: `weight_flags`: 1 marks a stored block of W, 0 an absent one; the share of stored blocks differs from block row to block row. `ham_flags`: 1 marks a stored block of the slab, 0 an absent one; the share of stored blocks differs from block row to block row.
All inputs are finite; a program needn't handle non-finite values.
Results may differ from a plain program's by a relative error of at most 0.001.
Values may be sent and summed in bfloat16 or wider, within the bound.
A program may use at most 64 MiB of HBM per device.

v0:
```python
import functools

import jax
import jax.numpy as jnp
from jax import lax
from jax.experimental import pallas as pl
from jax.experimental.pallas import tpu as pltpu
from jax.sharding import PartitionSpec as P

STEPS = 4


def from_behind(block, axis, distance):
    devices = range(lax.axis_size(axis))
    route = [((i - distance) % len(devices), i) for i in devices]
    return lax.ppermute(block, axis, route)


def from_partner(value, axis, bit):
    mask = 2**bit
    pairs = [(source, source ^ mask) for source in range(lax.axis_size(axis))]
    return lax.ppermute(value, axis, pairs)


def masked(dense_tile, flag_grid):
    row_blocks, col_blocks = flag_grid.shape
    block_edge = dense_tile.shape[0] // row_blocks
    shaped = dense_tile.reshape(row_blocks, block_edge, col_blocks, block_edge)
    retain = (flag_grid > 0)[:, None, :, None]
    return jnp.where(retain, shaped, jnp.zeros_like(shaped)).reshape(dense_tile.shape)


def aligned(operand, amount, bit_count, mover):
    for level in range(bit_count):
        moved = mover(operand, level)
        chosen = (amount >> level) % 2 == 1
        operand = jnp.where(chosen, moved, operand)
    return operand


def contract(left_part, right_part):
    return lax.dot_general(
        left_part, right_part, (((0,), (0,)), ((), ())), preferred_element_type=jnp.float32
    )


def shards(weights, weight_flags, hamiltonian, ham_flags):
    row_count = lax.axis_size("row")
    bit_count = (row_count - 1).bit_length()
    row_index = lax.axis_index("row")
    col_index = lax.axis_index("col")
    pair_index = col_index // 2
    parity = col_index % 2
    w_masked = masked(weights, weight_flags)
    h_masked = masked(hamiltonian, ham_flags)
    ham_tile = aligned(
        h_masked,
        pair_index,
        bit_count,
        lambda operand, level: from_behind(operand, "row", -(1 << level)),
    )
    w_half = aligned(
        w_masked,
        row_index,
        bit_count,
        lambda operand, level: from_behind(operand, "col", -(2 << level)),
    )
    half_rows = ham_tile.shape[0] // 2
    upper_rows = ham_tile[:half_rows]
    lower_rows = ham_tile[half_rows:]
    retained = jnp.where(parity == 0, upper_rows, lower_rows)
    handed = jnp.where(parity == 0, lower_rows, upper_rows)
    received = from_partner(handed, "col", 0)
    joined = jnp.where(
        parity == 0,
        jnp.concatenate((retained, received), 1),
        jnp.concatenate((received, retained), 1),
    )
    summed = contract(w_half, joined)
    for step_index in range(1, STEPS):
        w_half = from_behind(w_half, "col", -2)
        joined = from_behind(joined, "row", -1)
        summed = summed + contract(w_half, joined)
    half_width = summed.shape[1] // 2
    own_part = jnp.where(parity == 0, summed[:, :half_width], summed[:, half_width:])
    their_part = jnp.where(parity == 0, summed[:, half_width:], summed[:, :half_width])
    summed = own_part + from_partner(their_part, "col", 0)
    return summed.astype(jnp.bfloat16)


SHARES = (5, 3)
CHUNKS = len(SHARES)
MESH = pl.DeviceIdType.MESH


def put(source, target, sent, landed, device):
    return pltpu.make_async_remote_copy(
        src_ref=source,
        dst_ref=target,
        send_sem=sent,
        recv_sem=landed,
        device_id=device,
        device_id_type=MESH,
    )


def gather_kernel(
    panels, w_flags_hbm, h_flags_hbm, w_hbm, h_hbm, out_ref, w_flags, h_flags, w_ref, h_ref, w_buf, h_buf, total,
    loaded, w_landed, up_sent, down_sent, core_sent, h_landed, h_sent,
):
    row = lax.axis_index("row")
    col = lax.axis_index("col")
    pair = col // 2
    core = col % 2
    partner = (row, pair * 2 + 1 - core)
    above = (row, col + 2)
    below = (row, col - 2)
    beside = row + 1 - 2 * (row % 2)
    across = (row + panels // 2) % panels
    opposite = (beside + panels // 2) % panels
    has_above = pair < panels - 1
    has_below = pair > 0

    loads = [
        pltpu.make_async_copy(source, target, loaded.at[n])
        for n, (source, target) in enumerate(
            ((w_flags_hbm, w_flags), (w_hbm, w_ref), (h_flags_hbm, h_flags), (h_hbm, h_ref))
        )
    ]
    for load in loads:
        load.start()

    barrier = pltpu.get_barrier_semaphore()

    def greet(device):
        pl.semaphore_signal(barrier, inc=1, device_id=device, device_id_type=MESH)

    greet(partner)
    greet((beside, col))
    greet((across, col))

    @pl.when(has_above)
    def _():
        greet(above)

    @pl.when(has_below)
    def _():
        greet(below)

    loads[0].wait()
    loads[1].wait()
    half_rows, width = w_ref.shape
    edge = half_rows // w_flags.shape[0]
    bounds = [half_rows * sum(SHARES[:k]) // sum(SHARES) for k in range(CHUNKS + 1)]
    for r in range(w_flags.shape[0]):
        for c in range(w_flags.shape[1]):
            rows, lanes = slice(r * edge, (r + 1) * edge), slice(c * edge, (c + 1) * edge)
            block = w_ref[rows, lanes]
            kept = jnp.where(w_flags[r, c] > 0, block, jnp.zeros_like(block))
            w_buf[pair, core, rows, lanes] = kept
    pl.semaphore_wait(
        barrier, 3 + has_above.astype(jnp.int32) + has_below.astype(jnp.int32)
    )

    def piece(k):
        return slice(bounds[k], bounds[k + 1])

    def go_up(panel, k):
        slot = w_buf.at[panel, core, piece(k)]
        return put(slot, slot, up_sent.at[panel, k], w_landed.at[panel, core, k], above)

    def go_down(panel, k):
        slot = w_buf.at[panel, core, piece(k)]
        return put(slot, slot, down_sent.at[panel, k], w_landed.at[panel, core, k], below)

    def go_over(panel, k):
        slot = w_buf.at[panel, core, piece(k)]
        return put(slot, slot, core_sent.at[panel, k], w_landed.at[panel, core, k], partner)

    def arrival(panel, half, k):
        slot = w_buf.at[panel, half, piece(k)]
        return put(slot, slot, core_sent.at[panel, k], w_landed.at[panel, half, k], partner)

    def h_put(panel, half, number, device):
        slot = h_buf.at[panel, half]
        return put(slot, slot, h_sent.at[number], h_landed.at[panel, half], device)

    def each(body):
        for k in range(CHUNKS):
            body(k)

    def first_sends(k):
        @pl.when(has_above)
        def _():
            go_up(pair, k).start()

        @pl.when(has_below)
        def _():
            go_down(pair, k).start()

    each(first_sends)
    loads[2].wait()
    loads[3].wait()
    for r in range(h_flags.shape[1]):
        for c in range(h_flags.shape[0]):
            lanes = slice(c * edge, (c + 1) * edge)
            block = h_ref[r * edge:(r + 1) * edge, lanes]
            half, start = divmod(r * edge, half_rows)
            kept = jnp.where(h_flags[c, r] > 0, block, jnp.zeros_like(block))
            h_buf[row, half, start:start + edge, lanes] = kept

    h_copies = [
        h_put(row, 0, 0, (beside, col)),
        h_put(row, 1, 1, (across, col)),
        h_put(row, 1, 2, (beside, col)),
        h_put(row, 0, 3, (across, col)),
    ]
    for copy in h_copies:
        copy.start()
    each(lambda k: go_over(pair, k).start())

    def relay(distance, k):
        @pl.when(pair >= distance)
        def _():
            panel = pair - distance
            arrival(panel, core, k).wait_recv()

            @pl.when(has_above)
            def _():
                go_up(panel, k).start()

            go_over(panel, k).start()

        @pl.when(pair + distance < panels)
        def _():
            panel = pair + distance
            arrival(panel, core, k).wait_recv()

            @pl.when(has_below)
            def _():
                go_down(panel, k).start()

            go_over(panel, k).start()

    each(functools.partial(relay, 1))
    h_put(beside, 0, 0, (beside, col)).wait_recv()
    relay_across = h_put(beside, 0, 4, (across, col))
    relay_across.start()
    h_put(across, 1, 0, (beside, col)).wait_recv()
    relay_beside = h_put(across, 1, 5, (beside, col))
    relay_beside.start()
    for distance in range(2, panels - 1):
        each(functools.partial(relay, distance))
    h_put(beside, 1, 0, (beside, col)).wait_recv()
    h_put(across, 0, 0, (beside, col)).wait_recv()
    h_put(opposite, 0, 0, (beside, col)).wait_recv()
    h_put(opposite, 1, 0, (beside, col)).wait_recv()

    total[...] = jnp.zeros_like(total)
    span = 2 * half_rows

    def near_panel(step, carry):
        panel = (pair + step) % panels
        gap = panel - pair

        @pl.when((gap < panels - 1) & (gap > 1 - panels))
        def _():
            each(lambda k: arrival(panel, 1 - core, k).wait_recv())
            left = w_buf[panel].reshape(span, width)
            right = h_buf[panel].reshape(span, h_buf.shape[3])
            total[...] += contract(left, right)

        return carry

    lax.fori_loop(0, panels, near_panel, 0)

    is_end = (pair == 0) | (pair == panels - 1)

    @pl.when(is_end)
    def _():
        panel = panels - 1 - pair

        def product(half, k):
            return contract(w_buf[panel, half, piece(k)], h_buf[panel, half, piece(k)])

        for k in range(CHUNKS - 1):
            arrival(panel, core, k).wait_recv()
            go_over(panel, k).start()
            total[...] += product(core, k)
            arrival(panel, 1 - core, k).wait_recv()
            total[...] += product(1 - core, k)

        last = CHUNKS - 1
        arrival(panel, core, last).wait_recv()
        go_over(panel, last).start()
        total[...] += product(core, last)
        arrival(panel, 1 - core, last).wait_recv()
        out_ref[...] = (total[...] + product(1 - core, last)).astype(out_ref.dtype)

    @pl.when(jnp.logical_not(is_end))
    def _():
        out_ref[...] = total[...].astype(out_ref.dtype)

    for copy in h_copies + [relay_across, relay_beside]:
        copy.wait_send()

    def drain(panel, carry):
        def one(k):
            go_over(panel, k).wait_send()

            @pl.when(has_above & (panel <= pair))
            def _():
                go_up(panel, k).wait_send()

            @pl.when(has_below & (panel >= pair))
            def _():
                go_down(panel, k).wait_send()

        each(one)
        return carry

    lax.fori_loop(0, panels, drain, 0)


def gathered(weights, weight_flags, hamiltonian, ham_flags):
    panels = lax.axis_size("row")
    half_rows, width = weights.shape
    panel_rows, slice_cols = hamiltonian.shape
    dma = pltpu.SemaphoreType.DMA
    vmem = pl.BlockSpec(memory_space=pltpu.VMEM)
    hbm = pl.BlockSpec(memory_space=pl.ANY)
    return pl.pallas_call(
        functools.partial(gather_kernel, panels),
        out_shape=pltpu.VMEM((width, slice_cols), jnp.bfloat16),
        in_specs=[hbm] * 4,
        out_specs=vmem,
        scratch_shapes=[
            pltpu.SMEM(weight_flags.shape, weight_flags.dtype),
            pltpu.SMEM(ham_flags.shape[::-1], ham_flags.dtype),
            pltpu.VMEM(weights.shape, weights.dtype),
            pltpu.VMEM(hamiltonian.shape, hamiltonian.dtype),
            pltpu.VMEM((panels, 2, half_rows, width), jnp.bfloat16),
            pltpu.VMEM((panels, 2, panel_rows // 2, slice_cols), jnp.bfloat16),
            pltpu.VMEM((width, slice_cols), jnp.float32),
            dma((4,)),
            dma((panels, 2, CHUNKS)),
            dma((panels, CHUNKS)),
            dma((panels, CHUNKS)),
            dma((panels, CHUNKS)),
            dma((panels, 2)),
            dma((6,)),
        ],
        compiler_params=pltpu.CompilerParams(collective_id=0, has_side_effects=True),
    )(weight_flags, ham_flags.T, weights, hamiltonian)


def solution(mesh):
    placed = (P("col", "row"), P("col", "row"), P("row", "col"), P("row", "col"))
    every_panel = mesh.shape["row"] == STEPS and mesh.shape["col"] == 2 * STEPS
    return jax.shard_map(
        gathered if every_panel else shards,
        mesh=mesh, in_specs=placed, out_specs=P("row", "col"), check_vma=False,
    )
```

profile of v0, /device:TPU:0, one launch (start us, length us, event | category | flops | bytes accessed | tf_op | source)
XLA Modules:
  0.0 45.5 jit_solution(4442482580952085528)
XLA Ops:
  0.0 44.6 %shard_map.46 = bf16[768,512]{1,0:T(8,128)(2,1)S(1)} custom-call(s32[3,6]{1,0:T(4,128)} %w_flags_hbm.1, s32[4,6]{1,0:T(4,128)} %bitcast.1, bf16[384,768]{1,0:T(8,128)(2,1)} %w_hbm.1, bf16[768,512]{1,0:T(8,128)(2,1)} %h_hbm.1), custom_call_target="tpu_custom_call" | custom-call | tf_op jit(solution)/shard_map/pallas_call | solution.py:332
  44.6 0.9 %copy.6 = bf16[768,512]{1,0:T(8,128)(2,1)} copy(bf16[768,512]{1,0:T(8,128)(2,1)S(1)} %shard_map.46) | data formatting | bytes 1572864
where the time goes:
time: 46 us; the launch traced here: 45.5 us
  Pallas kernels  44.6 us (97%)
  local copies, waits for them, and re-layouts  0.88 us (2%)
    pallas_call x1, Pallas kernels, gathered(): pl.pallas_call(functools.partial(gather_kernel, panels), out_shape=pltpu....  44.6 us

commit v1 on v0

--- a/solution.py
+++ b/solution.py
@@ -354,10 +354,603 @@
     )(weight_flags, ham_flags.T, weights, hamiltonian)
 
 
+def packed_kernel(
+    panels, w_flags_hbm, h_flags_hbm, w_hbm, h_hbm, out_ref, over_ref,
+    h_flags, same_flags, other_flags, first_from, spill, starts, totals, line_over,
+    w_blocks, h_ref, same, other, from_above, from_below, to_below, to_above, w_buf, h_buf, total,
+    loaded, same_landed, other_landed, down_sent, up_sent, core_sent,
+    shared_landed, shared_sent, shared_core_sent, h_landed, h_sent, over_landed, over_sent,
+):
+    row = lax.axis_index("row")
+    col = lax.axis_index("col")
+    pair = col // 2
+    core = col % 2
+    partner = (row, pair * 2 + 1 - core)
+    above = (row, col + 2)
+    below = (row, col - 2)
+    beside = row + 1 - 2 * (row % 2)
+    across = (row + panels // 2) % panels
+    opposite = (beside + panels // 2) % panels
+    top = panels - 1
+    has_above = pair < top
+    has_below = pair > 0
+    home = top
+    w_flags = same_flags[home]
+    row_blocks, col_blocks = w_flags.shape
+    blocks, edge = w_blocks.shape[0], w_blocks.shape[1]
+    half_rows = row_blocks * edge
+    shared = from_above.shape[0]
+    part = shared // 2
+    base = base_slots(blocks)
+    early = early_slots(blocks)
+    rest = blocks - base
+    slices = (slice(0, early), slice(early, base))
+    FLAGS, WHOLE = 2, 0
+
+    flag_load = pltpu.make_async_copy(w_flags_hbm, w_flags, loaded.at[0])
+    flag_load.start()
+    w_loads = []
+    for b in range(blocks):
+        r, c = divmod(b, col_blocks)
+        source = w_hbm.at[r * edge:(r + 1) * edge, c * edge:(c + 1) * edge]
+        load = pltpu.make_async_copy(source, w_blocks.at[b], loaded.at[3 + b])
+        load.start()
+        w_loads.append(load)
+    h_loads = [
+        pltpu.make_async_copy(h_flags_hbm, h_flags, loaded.at[1]),
+        pltpu.make_async_copy(h_hbm, h_ref, loaded.at[2]),
+    ]
+    for load in h_loads:
+        load.start()
+
+    barrier = pltpu.get_barrier_semaphore()
+
+    def greet(device):
+        pl.semaphore_signal(barrier, inc=1, device_id=device, device_id_type=MESH)
+
+    greet(partner)
+    greet((beside, col))
+    greet((across, col))
+
+    @pl.when(has_above)
+    def _():
+        greet(above)
+
+    @pl.when(has_below)
+    def _():
+        greet(below)
+
+    def piece(refs, flags, o, k):
+        return flags[o] if k == FLAGS else refs[o].at[slices[k]]
+
+    def go_down(d, k):
+        source, target = (piece(same, same_flags, home + n, k) for n in (d, d + 1))
+        return put(source, target, down_sent.at[d, k], same_landed.at[home + d + 1, k], below)
+
+    def go_up(d, k):
+        source, target = (piece(same, same_flags, home - n, k) for n in (d, d + 1))
+        return put(source, target, up_sent.at[d, k], same_landed.at[home - d - 1, k], above)
+
+    def go_over(o, k):
+        if o == home and k == WHOLE:
+            source, target = same[o], other[o]
+        else:
+            source, target = piece(same, same_flags, o, k), piece(other, other_flags, o, k)
+        return put(source, target, core_sent.at[o, k], other_landed.at[o, k], partner)
+
+    def landed(o, k):
+        slot = piece(same, same_flags, o, k)
+        return put(slot, slot, core_sent.at[o, k], same_landed.at[o, k], partner)
+
+    def crossed(o, k):
+        return go_over(o, k)
+
+    def shared_half(ref, half):
+        return ref.at[pl.ds(half * part, part)]
+
+    def shared_down():
+        return put(to_below, shared_half(from_above, core), shared_sent.at[0], shared_landed.at[0, 0], below)
+
+    def shared_up():
+        return put(to_above, shared_half(from_below, core), shared_sent.at[1], shared_landed.at[1, 0], above)
+
+    def shared_over(side):
+        slot = shared_half((from_above, from_below)[side], core)
+        return put(slot, slot, shared_core_sent.at[side], shared_landed.at[side, 1], partner)
+
+    def shared_arrival(side):
+        slot = shared_half((from_above, from_below)[side], core)
+        return put(slot, slot, shared_core_sent.at[side], shared_landed.at[side, 0], partner)
+
+    def shared_crossed(side):
+        slot = shared_half((from_above, from_below)[side], 1 - core)
+        return put(slot, slot, shared_core_sent.at[side], shared_landed.at[side, 1], partner)
+
+    def h_put(panel, half, number, device):
+        slot = h_buf.at[panel, half]
+        return put(slot, slot, h_sent.at[number], h_landed.at[panel, half], device)
+
+    flag_load.wait()
+    nearest = jnp.int32(blocks - 1)
+    first_from[blocks] = nearest
+    for b in reversed(range(blocks)):
+        nearest = jnp.where(w_flags[divmod(b, col_blocks)] > 0, b, nearest)
+        first_from[b] = nearest
+    for load in w_loads:
+        load.wait()
+
+    def pack(start, stop, chosen):
+        for k in range(start, stop):
+            same[home][k] = w_blocks[chosen]
+            chosen = first_from[chosen + 1]
+        return chosen
+
+    chosen = pack(0, early, first_from[0])
+    pl.semaphore_wait(
+        barrier, 3 + has_above.astype(jnp.int32) + has_below.astype(jnp.int32)
+    )
+
+    def both_ways(k, down, up):
+        @pl.when(down)
+        def _():
+            go_down(0, k).start()
+
+        @pl.when(up)
+        def _():
+            go_up(0, k).start()
+
+    both_ways(0, has_below, has_above)
+    both_ways(FLAGS, has_below, has_above)
+    go_over(home, FLAGS).start()
+    chosen = pack(early, base, chosen)
+    both_ways(1, has_below & (pair < top), has_above & (pair > 0))
+    pack(base, blocks, chosen)
+    go_over(home, WHOLE).start()
+
+    for load in h_loads:
+        load.wait()
+    for r in range(h_flags.shape[1]):
+        for c in range(h_flags.shape[0]):
+            lanes = slice(c * edge, (c + 1) * edge)
+            block = h_ref[r * edge:(r + 1) * edge, lanes]
+            half, start = divmod(r * edge, half_rows)
+            kept = jnp.where(h_flags[c, r] > 0, block, jnp.zeros_like(block))
+            h_buf[row, half, start:start + edge, lanes] = kept
+
+    h_copies = [
+        h_put(row, 0, 0, (beside, col)),
+        h_put(row, 1, 1, (across, col)),
+        h_put(row, 1, 2, (beside, col)),
+        h_put(row, 0, 3, (across, col)),
+    ]
+    for copy in h_copies:
+        copy.start()
+
+    def beyond(flags):
+        count = jnp.int32(0)
+        for r in range(row_blocks):
+            for c in range(col_blocks):
+                count = count + (flags[r, c] > 0).astype(jnp.int32)
+        return jnp.maximum(count - base, 0)
+
+    crossed(home, FLAGS).wait_recv()
+    own_same = beyond(w_flags)
+    own_other = beyond(other_flags[home])
+    own_both = own_same + own_other
+    same_start = jnp.where(core == 0, 0, own_other)
+    other_start = jnp.where(core == 0, own_same, 0)
+
+    def within(index, limit):
+        return jnp.minimum(jnp.maximum(index, 0), limit - 1)
+
+    def share(target, source):
+        for n in range(part):
+            slot = core * part + n
+            in_same, in_other = slot - same_start, slot - other_start
+            value = other[home][base + within(in_other, rest)]
+            if source is not None:
+                passed = source[within(slot - own_both, shared)]
+                value = jnp.where((in_other >= 0) & (in_other < own_other), value, passed)
+            mine = same[home][base + within(in_same, rest)]
+            target[n] = jnp.where((in_same >= 0) & (in_same < own_same), mine, value)
+
+    crossed(home, WHOLE).wait_recv()
+
+    @pl.when(pair == top)
+    def _():
+        share(to_below, None)
+        shared_down().start()
+        go_down(0, 1).start()
+
+    @pl.when(pair == 0)
+    def _():
+        share(to_above, None)
+        shared_up().start()
+        go_up(0, 1).start()
+
+    def dense(flags, packed, panel, half):
+        position = jnp.int32(0)
+        for r in range(row_blocks):
+            for c in range(col_blocks):
+                block = packed[position]
+                present = flags[r, c] > 0
+                rows, lanes = slice(r * edge, (r + 1) * edge), slice(c * edge, (c + 1) * edge)
+                w_buf[panel, half, rows, lanes] = jnp.where(present, block, jnp.zeros_like(block))
+                position = position + present.astype(jnp.int32)
+
+    dense(w_flags, same[home], pair, core)
+    dense(other_flags[home], other[home], pair, 1 - core)
+    total[...] = jnp.zeros_like(total)
+
+    def forward(d, k):
+        @pl.when(pair + d <= top)
+        def _():
+            landed(home + d, k).wait_recv()
+
+            @pl.when(has_below)
+            def _():
+                go_down(d, k).start()
+
+            go_over(home + d, k).start()
+
+        @pl.when(pair - d >= 0)
+        def _():
+            landed(home - d, k).wait_recv()
+
+            @pl.when(has_above)
+            def _():
+                go_up(d, k).start()
+
+            go_over(home - d, k).start()
+
+    def receive(d, k):
+        @pl.when(pair + d <= top)
+        def _():
+            landed(home + d, k).wait_recv()
+            go_over(home + d, k).start()
+
+        @pl.when(pair - d >= 0)
+        def _():
+            landed(home - d, k).wait_recv()
+            go_over(home - d, k).start()
+
+    def middle(d):
+        @pl.when(pair + d < top)
+        def _():
+            landed(home + d, 1).wait_recv()
+
+            @pl.when(has_below)
+            def _():
+                go_down(d, 1).start()
+
+            go_over(home + d, 1).start()
+
+        @pl.when(pair - d > 0)
+        def _():
+            landed(home - d, 1).wait_recv()
+
+            @pl.when(has_above)
+            def _():
+                go_up(d, 1).start()
+
+            go_over(home - d, 1).start()
+
+    def last(d):
+        @pl.when(pair + d == top)
+        def _():
+            shared_arrival(0).wait_recv()
+            shared_over(0).start()
+            shared_crossed(0).wait_recv()
+
+            @pl.when(has_below)
+            def _():
+                share(to_below, from_above)
+                shared_down().start()
+
+            landed(home + d, 1).wait_recv()
+
+            @pl.when(has_below)
+            def _():
+                go_down(d, 1).start()
+
+            go_over(home + d, 1).start()
+
+        @pl.when(pair - d == 0)
+        def _():
+            shared_arrival(1).wait_recv()
+            shared_over(1).start()
+            shared_crossed(1).wait_recv()
+
+            @pl.when(has_above)
+            def _():
+                share(to_above, from_below)
+                shared_up().start()
+
+            landed(home - d, 1).wait_recv()
+
+            @pl.when(has_above)
+            def _():
+                go_up(d, 1).start()
+
+            go_over(home - d, 1).start()
+
+    forward(1, FLAGS)
+    forward(1, 0)
+    h_put(beside, 0, 0, (beside, col)).wait_recv()
+    relay_across = h_put(beside, 0, 4, (across, col))
+    relay_across.start()
+    h_put(across, 1, 0, (beside, col)).wait_recv()
+    relay_beside = h_put(across, 1, 5, (beside, col))
+    relay_beside.start()
+    middle(1)
+    forward(2, FLAGS)
+    last(1)
+    forward(2, 0)
+    receive(3, FLAGS)
+    middle(2)
+
+    totals[0] = jnp.where(pair > 0, own_both, 0)
+    totals[1] = jnp.where(pair < top, own_both, 0)
+    for side, way in ((0, 1), (1, -1)):
+        starts[home, side] = jnp.int32(0)
+        for d in range(1, panels):
+            o, n = home + way * d, pair + way * d
+
+            @pl.when((n >= 0) & (n <= top))
+            def _(o=o, n=n, side=side):
+                crossed(o, FLAGS).wait_recv()
+                at_same, at_other = beyond(same_flags[o]), beyond(other_flags[o])
+                start = starts[home, side]
+                starts[o, 0] = start + jnp.where(core == 0, 0, at_other)
+                starts[o, 1] = start + jnp.where(core == 0, at_same, 0)
+                starts[home, side] = start + at_same + at_other
+                totals[0] += jnp.where(n > 0, at_same + at_other, 0)
+                totals[1] += jnp.where(n < top, at_same + at_other, 0)
+
+    line_over[0, 0] = jnp.maximum(totals[0] - shared, 0) + jnp.maximum(totals[1] - shared, 0)
+
+    def agree(n, device):
+        return put(line_over.at[2 * n], line_over.at[2 * n + 1], over_sent.at[n], over_landed.at[n], device)
+
+    agree(0, (beside, col)).start()
+    last(2)
+    agree(0, (beside, col)).wait_recv()
+    line_over[2, 0] = line_over[0, 0] + line_over[1, 0]
+    agree(1, (across, col)).start()
+
+    def fill(o, side):
+        source = (from_above, from_below)[side]
+        for n in range(rest):
+            same[o][base + n] = source[within(starts[o, 0] + n, shared)]
+            other[o][base + n] = source[within(starts[o, 1] + n, shared)]
+
+    def spread(o, way_d):
+        dense(same_flags[o], same[o], pair + way_d, core)
+        dense(other_flags[o], other[o], pair + way_d, 1 - core)
+
+    h_put(beside, 1, 0, (beside, col)).wait_recv()
+    h_put(across, 0, 0, (beside, col)).wait_recv()
+    far = top
+
+    @pl.when(pair + far == top)
+    def _():
+        landed(home + far, 0).wait_recv()
+        go_over(home + far, 0).start()
+        shared_arrival(0).wait_recv()
+        shared_over(0).start()
+
+    @pl.when(pair - far == 0)
+    def _():
+        landed(home - far, 0).wait_recv()
+        go_over(home - far, 0).start()
+        shared_arrival(1).wait_recv()
+        shared_over(1).start()
+
+    h_put(opposite, 0, 0, (beside, col)).wait_recv()
+    h_put(opposite, 1, 0, (beside, col)).wait_recv()
+    span = 2 * half_rows
+    width = col_blocks * edge
+
+    def add(panel):
+        left = w_buf[panel].reshape(span, width)
+        right = h_buf[panel].reshape(span, h_buf.shape[3])
+        total[...] += contract(left, right)
+
+    def one_panel(step, carry):
+        add((pair + step) % panels)
+        return carry
+
+    add(pair)
+
+    @pl.when(pair + far == top)
+    def _():
+        shared_crossed(0).wait_recv()
+
+    @pl.when(pair - far == 0)
+    def _():
+        shared_crossed(1).wait_recv()
+
+    for side, way in ((0, 1), (1, -1)):
+        for d in range(1, far):
+            o, n = home + way * d, pair + way * d
+
+            @pl.when((n >= 0) & (n <= top))
+            def _(o=o, side=side, way=way, d=d):
+                for k in range(2):
+                    crossed(o, k).wait_recv()
+                fill(o, side)
+                spread(o, way * d)
+
+    def near_panel(step, carry):
+        panel = (pair + step) % panels
+        gap = panel - pair
+
+        @pl.when((gap < far) & (gap > -far))
+        def _():
+            add(panel)
+
+        return carry
+
+    lax.fori_loop(1, panels, near_panel, 0)
+
+    is_end = (pair == 0) | (pair == top)
+    for side, way in ((0, 1), (1, -1)):
+        o = home + way * far
+
+        @pl.when(pair == (0, top)[side])
+        def _(o=o, side=side, way=way):
+            landed(o, 1).wait_recv()
+            go_over(o, 1).start()
+            crossed(o, 0).wait_recv()
+            fill(o, side)
+            dense(same_flags[o], same[o], pair + way * far, core)
+
+    @pl.when(is_end)
+    def _():
+        panel = top - pair
+        total[...] += contract(w_buf[panel, core], h_buf[panel, core])
+
+    for side, way in ((0, 1), (1, -1)):
+        o = home + way * far
+
+        @pl.when(pair == (0, top)[side])
+        def _(o=o, side=side, way=way):
+            crossed(o, 1).wait_recv()
+            dense(other_flags[o], other[o], pair + way * far, 1 - core)
+
+    @pl.when(is_end)
+    def _():
+        panel = top - pair
+        final = total[...] + contract(w_buf[panel, 1 - core], h_buf[panel, 1 - core])
+        out_ref[...] = final.astype(out_ref.dtype)
+
+    @pl.when(jnp.logical_not(is_end))
+    def _():
+        out_ref[...] = total[...].astype(out_ref.dtype)
+
+    agree(1, (across, col)).wait_recv()
+    over_ref[0, 0] = line_over[2, 0] + line_over[3, 0]
+    for n in range(2):
+        agree(n, (beside, col)).wait_send()
+    for copy in h_copies + [relay_across, relay_beside]:
+        copy.wait_send()
+    go_over(home, FLAGS).wait_send()
+    go_over(home, WHOLE).wait_send()
+
+    @pl.when(has_above)
+    def _():
+        shared_over(0).wait_send()
+        shared_up().wait_send()
+
+    @pl.when(has_below)
+    def _():
+        shared_over(1).wait_send()
+        shared_down().wait_send()
+
+    for d in range(far):
+        @pl.when(has_below & (pair + d <= top))
+        def _(d=d):
+            for k in range(3):
+                go_down(d, k).wait_send()
+
+        @pl.when(has_above & (pair - d >= 0))
+        def _(d=d):
+            for k in range(3):
+                go_up(d, k).wait_send()
+
+    for d in range(1, panels):
+        @pl.when(pair + d <= top)
+        def _(d=d):
+            for k in range(3):
+                go_over(home + d, k).wait_send()
+
+        @pl.when(pair - d >= 0)
+        def _(d=d):
+            for k in range(3):
+                go_over(home - d, k).wait_send()
+
+
+def base_slots(blocks):
+    return 2 * blocks // 3
+
+
+def early_slots(blocks):
+    return 2 * base_slots(blocks) // 3
+
+
+def packed(weights, weight_flags, hamiltonian, ham_flags):
+    panels = lax.axis_size("row")
+    half_rows, width = weights.shape
+    panel_rows, slice_cols = hamiltonian.shape
+    edge = half_rows // weight_flags.shape[0]
+    blocks = weight_flags.size
+    shared = base_slots(blocks)
+    offsets = 2 * panels - 1
+    dma = pltpu.SemaphoreType.DMA
+    hbm = pl.BlockSpec(memory_space=pl.ANY)
+
+    def many(shape, dtype, space):
+        return [space(shape, dtype) for _ in range(offsets)]
+
+    def slots(count):
+        return pltpu.VMEM((count, edge, edge), jnp.bfloat16)
+
+    out, over = pl.pallas_call(
+        functools.partial(packed_kernel, panels),
+        out_shape=(
+            pltpu.VMEM((width, slice_cols), jnp.bfloat16),
+            jax.ShapeDtypeStruct((1, 1), jnp.int32),
+        ),
+        in_specs=[hbm] * 4,
+        out_specs=(pl.BlockSpec(memory_space=pltpu.VMEM), pl.BlockSpec(memory_space=pltpu.SMEM)),
+        scratch_shapes=[
+            pltpu.SMEM(ham_flags.shape[::-1], ham_flags.dtype),
+            many(weight_flags.shape, weight_flags.dtype, pltpu.SMEM),
+            many(weight_flags.shape, weight_flags.dtype, pltpu.SMEM),
+            pltpu.SMEM((blocks + 1,), jnp.int32),
+            pltpu.SMEM((offsets, 2), jnp.int32),
+            pltpu.SMEM((offsets, 2), jnp.int32),
+            pltpu.SMEM((2,), jnp.int32),
+            pltpu.SMEM((4, 1), jnp.int32),
+            slots(blocks),
+            pltpu.VMEM(hamiltonian.shape, hamiltonian.dtype),
+            [slots(blocks) for _ in range(offsets)],
+            [slots(blocks) for _ in range(offsets)],
+            slots(shared),
+            slots(shared),
+            slots(shared // 2),
+            slots(shared // 2),
+            pltpu.VMEM((panels, 2, half_rows, width), jnp.bfloat16),
+            pltpu.VMEM((panels, 2, panel_rows // 2, slice_cols), jnp.bfloat16),
+            pltpu.VMEM((width, slice_cols), jnp.float32),
+            dma((3 + blocks,)),
+            dma((offsets, 3)),
+            dma((offsets, 3)),
+            dma((panels, 3)),
+            dma((panels, 3)),
+            dma((offsets, 3)),
+            dma((2, 2)),
+            dma((2,)),
+            dma((2,)),
+            dma((panels, 2)),
+            dma((6,)),
+            dma((2,)),
+            dma((2,)),
+        ],
+        compiler_params=pltpu.CompilerParams(collective_id=1, has_side_effects=True),
+    )(weight_flags, ham_flags.T, weights, hamiltonian)
+    return lax.cond(
+        over[0, 0] > 0,
+        lambda kept, *given: gathered(*given),
+        lambda kept, *given: kept,
+        out, weights, weight_flags, hamiltonian, ham_flags,
+    )
+
+
 def solution(mesh):
     placed = (P("col", "row"), P("col", "row"), P("row", "col"), P("row", "col"))
     every_panel = mesh.shape["row"] == STEPS and mesh.shape["col"] == 2 * STEPS
     return jax.shard_map(
-        gathered if every_panel else shards,
+        packed if every_panel else shards,
         mesh=mesh, in_specs=placed, out_specs=P("row", "col"), check_vma=False,
     )

time: 46 us -> 43 us (0.935)
  Pallas kernels: 44.6 us -> 39.9 us
  local copies, waits for them, and re-layouts: 0.88 us -> 2.22 us
  between operations: 0.01 us -> 0.73 us
    pallas_call x1, Pallas kernels: 44.6 us -> 39.9 us  [packed(): pl.pallas_call(functools.partial(packed_kernel, panels), out_shape=(pltpu...]
    unnamed x1 -> x9, local copies, waits for them, and re-layouts: 0.88 us -> 2.22 us
where the time goes in v1:
time: 43 us; the launch traced here: 42.9 us
  Pallas kernels  39.9 us (93%)
  local copies, waits for them, and re-layouts  2.22 us (5%)
  between operations  0.73 us (2%)
    pallas_call x1, Pallas kernels, packed(): pl.pallas_call(functools.partial(packed_kernel, panels), out_shape=(pltpu...  39.9 us
    unnamed x9, local copies, waits for them, and re-layouts  2.22 us

profile of v1, /device:TPU:0, one launch (start us, length us, event | category | flops | bytes accessed | tf_op | source)
XLA Modules:
  0.0 42.9 jit_solution(7057894089263357401)
XLA Ops:
  0.0 0.0 copy-start.3
  0.0 0.0 copy-start
  0.0 0.7 %copy-done.3 = s32[6,4]{0,1:T(4,128)S(1)} copy-done((s32[6,4]{0,1:T(4,128)S(1)}, s32[6,4]{0,1:T(4,128)}, u32[]{:S(2)}) %copy-start.3) | copy-done | bytes 120
  0.7 0.0 copy-start.1
  0.7 39.9 %shard_map.48 = (bf16[768,512]{1,0:T(8,128)(2,1)S(1)}, s32[1,1]{1,0:T(1,128)}) custom-call(s32[3,6]{1,0:T(4,128)} %w_flags_hbm.1, s32[4,6]{1,0:T(4,128)S(1)} %bitcast.3, bf16[384,768]{1,0:T(8,128)(2,1)} %w_hbm.1, bf16[768,512]{1,0:T(8,128)(2,1)} %h_hbm.1), custom_call_target="tpu_custom_call" | custom-call | tf_op jit(solution)/shard_map/pallas_call | solution.py:898
  41.3 0.0 copy-start.2
  41.3 0.0 copy-done
  41.3 0.0 copy-done.1
  41.3 0.7 %copy-done.2 = s32[3,6]{1,0:T(4,128)S(1)} copy-done((s32[3,6]{1,0:T(4,128)S(1)}, s32[3,6]{1,0:T(4,128)}, u32[]{:S(2)}) %copy-start.2) | copy-done | bytes 96
  42.0 0.9 %copy.10 = bf16[768,512]{1,0:T(8,128)(2,1)} copy(bf16[768,512]{1,0:T(8,128)(2,1)S(1)} %get-tuple-element.25) | data formatting | bytes 1572864
  (1 shorter events, 0.0 us)
Async XLA Ops:
  0.0 0.7 %copy-start.3 = (s32[6,4]{0,1:T(4,128)S(1)}, s32[6,4]{0,1:T(4,128)}, u32[]{:S(2)}) copy-start(s32[6,4]{0,1:T(4,128)} %param.9) | copy-start | bytes 292
  0.0 41.3 %copy-start = (bf16[768,512]{1,0:T(8,128)(2,1)S(1)}, bf16[768,512]{1,0:T(8,128)(2,1)}, u32[]{:S(2)}) copy-start(bf16[768,512]{1,0:T(8,128)(2,1)} %h_hbm.1) | copy-start | bytes 2359300
  0.7 40.6 %copy-start.1 = (bf16[384,768]{1,0:T(8,128)(2,1)S(1)}, bf16[384,768]{1,0:T(8,128)(2,1)}, u32[]{:S(2)}) copy-start(bf16[384,768]{1,0:T(8,128)(2,1)} %w_hbm.1) | copy-start | bytes 1769476
  41.3 0.7 %copy-start.2 = (s32[3,6]{1,0:T(4,128)S(1)}, s32[3,6]{1,0:T(4,128)}, u32[]{:S(2)}) copy-start(s32[3,6]{1,0:T(4,128)} %w_flags_hbm.1) | copy-start | bytes 220

commit v2 on v1

--- a/solution.py
+++ b/solution.py
@@ -328,7 +328,7 @@
     panel_rows, slice_cols = hamiltonian.shape
     dma = pltpu.SemaphoreType.DMA
     vmem = pl.BlockSpec(memory_space=pltpu.VMEM)
-    hbm = pl.BlockSpec(memory_space=pl.ANY)
+    hbm = pl.BlockSpec(memory_space=pltpu.HBM)
     return pl.pallas_call(
         functools.partial(gather_kernel, panels),
         out_shape=pltpu.VMEM((width, slice_cols), jnp.bfloat16),
@@ -336,7 +336,7 @@
         out_specs=vmem,
         scratch_shapes=[
             pltpu.SMEM(weight_flags.shape, weight_flags.dtype),
-            pltpu.SMEM(ham_flags.shape[::-1], ham_flags.dtype),
+            pltpu.SMEM(ham_flags.shape, ham_flags.dtype),
             pltpu.VMEM(weights.shape, weights.dtype),
             pltpu.VMEM(hamiltonian.shape, hamiltonian.dtype),
             pltpu.VMEM((panels, 2, half_rows, width), jnp.bfloat16),
@@ -351,14 +351,14 @@
             dma((6,)),
         ],
         compiler_params=pltpu.CompilerParams(collective_id=0, has_side_effects=True),
-    )(weight_flags, ham_flags.T, weights, hamiltonian)
+    )(weight_flags, ham_flags, weights, hamiltonian)
 
 
 def packed_kernel(
     panels, w_flags_hbm, h_flags_hbm, w_hbm, h_hbm, out_ref, over_ref,
-    h_flags, same_flags, other_flags, first_from, spill, starts, totals, line_over,
-    w_blocks, h_ref, same, other, from_above, from_below, to_below, to_above, w_buf, h_buf, total,
-    loaded, same_landed, other_landed, down_sent, up_sent, core_sent,
+    h_flags, flags, places, first_from, starts, totals, line_over,
+    w_blocks, h_ref, same, other, late_same, late_other, from_above, from_below, to_below, to_above, w_buf, h_buf, total,
+    loaded, flags_landed, flags_down, flags_up, flags_core, same_landed, other_landed, down_sent, up_sent, core_sent,
     shared_landed, shared_sent, shared_core_sent, h_landed, h_sent, over_landed, over_sent,
 ):
     row = lax.axis_index("row")
@@ -375,27 +375,26 @@
     has_above = pair < top
     has_below = pair > 0
     home = top
-    w_flags = same_flags[home]
+    w_flags = flags[home].at[core]
     row_blocks, col_blocks = w_flags.shape
     blocks, edge = w_blocks.shape[0], w_blocks.shape[1]
     half_rows = row_blocks * edge
     shared = from_above.shape[0]
     part = shared // 2
     base = base_slots(blocks)
-    early = early_slots(blocks)
     rest = blocks - base
-    slices = (slice(0, early), slice(early, base))
-    FLAGS, WHOLE = 2, 0
+    slices = [slice(base * k // PIECES, base * (k + 1) // PIECES) for k in range(PIECES)]
+    final_piece = slices[-1]
+    WHOLE = 0
+    far = top
+    edges = (home - far, home + far)
 
     flag_load = pltpu.make_async_copy(w_flags_hbm, w_flags, loaded.at[0])
     flag_load.start()
-    w_loads = []
     for b in range(blocks):
         r, c = divmod(b, col_blocks)
         source = w_hbm.at[r * edge:(r + 1) * edge, c * edge:(c + 1) * edge]
-        load = pltpu.make_async_copy(source, w_blocks.at[b], loaded.at[3 + b])
-        load.start()
-        w_loads.append(load)
+        pltpu.make_async_copy(source, w_blocks.at[b], loaded.at[3]).start()
     h_loads = [
         pltpu.make_async_copy(h_flags_hbm, h_flags, loaded.at[1]),
         pltpu.make_async_copy(h_hbm, h_ref, loaded.at[2]),
@@ -420,30 +419,53 @@
     def _():
         greet(below)
 
-    def piece(refs, flags, o, k):
-        return flags[o] if k == FLAGS else refs[o].at[slices[k]]
+    def piece(refs, late, o, k):
+        if o in edges and k == PIECES - 1:
+            return late[edges.index(o)]
+        return refs[o].at[slices[k]]
+
+    def mark(o):
+        return (o - home) % panels - 1
 
     def go_down(d, k):
-        source, target = (piece(same, same_flags, home + n, k) for n in (d, d + 1))
-        return put(source, target, down_sent.at[d, k], same_landed.at[home + d + 1, k], below)
+        source, target = (piece(same, late_same, home + n, k) for n in (d, d + 1))
+        return put(source, target, down_sent.at[d], same_landed.at[mark(home + d + 1), k], below)
 
     def go_up(d, k):
-        source, target = (piece(same, same_flags, home - n, k) for n in (d, d + 1))
-        return put(source, target, up_sent.at[d, k], same_landed.at[home - d - 1, k], above)
+        source, target = (piece(same, late_same, home - n, k) for n in (d, d + 1))
+        return put(source, target, up_sent.at[d], same_landed.at[mark(home - d - 1), k], above)
 
     def go_over(o, k):
-        if o == home and k == WHOLE:
-            source, target = same[o], other[o]
-        else:
-            source, target = piece(same, same_flags, o, k), piece(other, other_flags, o, k)
-        return put(source, target, core_sent.at[o, k], other_landed.at[o, k], partner)
+        if o == home:
+            return put(same[o].at[:blocks], other[o].at[:blocks], core_sent.at[top], other_landed.at[top, 0], partner)
+        source, target = piece(same, late_same, o, k), piece(other, late_other, o, k)
+        return put(source, target, core_sent.at[mark(o)], other_landed.at[mark(o), k], partner)
+
+    def flags_go_down(d):
+        source, target = flags[home + d], flags[home + d + 1]
+        return put(source, target, flags_down.at[d], flags_landed.at[mark(home + d + 1)], below)
+
+    def flags_go_up(d):
+        source, target = flags[home - d], flags[home - d - 1]
+        return put(source, target, flags_up.at[d], flags_landed.at[mark(home - d - 1)], above)
+
+    def flags_arrival(o):
+        return put(flags[o], flags[o], flags_core.at[0], flags_landed.at[mark(o)], partner)
+
+    def flags_cross(half):
+        slot = flags[home].at[half]
+        return put(slot, slot, flags_core.at[0], flags_landed.at[top], partner)
 
     def landed(o, k):
-        slot = piece(same, same_flags, o, k)
-        return put(slot, slot, core_sent.at[o, k], same_landed.at[o, k], partner)
+        slot = piece(same, late_same, o, k)
+        return put(slot, slot, core_sent.at[0], same_landed.at[mark(o), k], partner)
 
     def crossed(o, k):
         return go_over(o, k)
+
+    def all_pieces(o, sent):
+        slot = same[o].at[:base]
+        return put(slot, slot, sent, same_landed.at[0, 0], partner)
 
     def shared_half(ref, half):
         return ref.at[pl.ds(half * part, part)]
@@ -466,18 +488,22 @@
         slot = shared_half((from_above, from_below)[side], 1 - core)
         return put(slot, slot, shared_core_sent.at[side], shared_landed.at[side, 1], partner)
 
-    def h_put(panel, half, number, device):
+    NEAR, OVER, FAR = 0, 1, 2
+
+    def h_put(panel, half, mark, sent, device):
         slot = h_buf.at[panel, half]
-        return put(slot, slot, h_sent.at[number], h_landed.at[panel, half], device)
+        return put(slot, slot, h_sent.at[sent], h_landed.at[mark, half], device)
+
+    def h_wait(panel, mark, half):
+        h_put(panel, half, mark, 0, (beside, col)).wait_recv()
 
     flag_load.wait()
     nearest = jnp.int32(blocks - 1)
     first_from[blocks] = nearest
     for b in reversed(range(blocks)):
-        nearest = jnp.where(w_flags[divmod(b, col_blocks)] > 0, b, nearest)
+        nearest = jnp.where(flags[home][core, b // col_blocks, b % col_blocks] > 0, b, nearest)
         first_from[b] = nearest
-    for load in w_loads:
-        load.wait()
+    pltpu.make_async_copy(same[home].at[:blocks], w_blocks, loaded.at[3]).wait()
 
     def pack(start, stop, chosen):
         for k in range(start, stop):
@@ -485,7 +511,7 @@
             chosen = first_from[chosen + 1]
         return chosen
 
-    chosen = pack(0, early, first_from[0])
+    chosen = pack(0, slices[0].stop, first_from[0])
     pl.semaphore_wait(
         barrier, 3 + has_above.astype(jnp.int32) + has_below.astype(jnp.int32)
     )
@@ -500,13 +526,9 @@
             go_up(0, k).start()
 
     both_ways(0, has_below, has_above)
-    both_ways(FLAGS, has_below, has_above)
-    go_over(home, FLAGS).start()
-    chosen = pack(early, base, chosen)
-    both_ways(1, has_below & (pair < top), has_above & (pair > 0))
-    pack(base, blocks, chosen)
+    flags_cross(core).start()
+    pack(slices[1].start, blocks, chosen)
     go_over(home, WHOLE).start()
-
     for load in h_loads:
         load.wait()
     for r in range(h_flags.shape[1]):
@@ -517,25 +539,35 @@
             kept = jnp.where(h_flags[c, r] > 0, block, jnp.zeros_like(block))
             h_buf[row, half, start:start + edge, lanes] = kept
 
-    h_copies = [
-        h_put(row, 0, 0, (beside, col)),
-        h_put(row, 1, 1, (across, col)),
-        h_put(row, 1, 2, (beside, col)),
-        h_put(row, 0, 3, (across, col)),
-    ]
-    for copy in h_copies:
-        copy.start()
-
-    def beyond(flags):
-        count = jnp.int32(0)
-        for r in range(row_blocks):
-            for c in range(col_blocks):
-                count = count + (flags[r, c] > 0).astype(jnp.int32)
-        return jnp.maximum(count - base, 0)
-
-    crossed(home, FLAGS).wait_recv()
-    own_same = beyond(w_flags)
-    own_other = beyond(other_flags[home])
+    h_put(row, 0, NEAR, 0, (beside, col)).start()
+    h_put(row, 1, OVER, 1, (across, col)).start()
+    h_put(row, 1, NEAR, 0, (beside, col)).start()
+    h_put(row, 0, OVER, 1, (across, col)).start()
+
+    flags_cross(1 - core).wait_recv()
+
+    @pl.when(has_below)
+    def _():
+        flags_go_down(0).start()
+
+    @pl.when(has_above)
+    def _():
+        flags_go_up(0).start()
+
+    for k in range(1, PIECES):
+        both_ways(k, has_below & (pair < top), has_above & (pair > 0))
+
+    def tabulate(o, which):
+        half = core if which == 0 else 1 - core
+        position = jnp.int32(0)
+        for b in range(blocks):
+            present = flags[o][half, b // col_blocks, b % col_blocks] > 0
+            places[2 * o + which, b] = jnp.where(present, position, blocks)
+            position = position + present.astype(jnp.int32)
+        return jnp.maximum(position - base, 0)
+
+    own_same = tabulate(home, 0)
+    own_other = tabulate(home, 1)
     own_both = own_same + own_other
     same_start = jnp.where(core == 0, 0, own_other)
     other_start = jnp.where(core == 0, own_same, 0)
@@ -560,26 +592,30 @@
     def _():
         share(to_below, None)
         shared_down().start()
-        go_down(0, 1).start()
+        for k in range(1, PIECES):
+            go_down(0, k).start()
 
     @pl.when(pair == 0)
     def _():
         share(to_above, None)
         shared_up().start()
-        go_up(0, 1).start()
-
-    def dense(flags, packed, panel, half):
-        position = jnp.int32(0)
-        for r in range(row_blocks):
+        for k in range(1, PIECES):
+            go_up(0, k).start()
+
+    def dense(o, which, panel, wanted):
+        packed = (same, other)[which][o]
+        half = core if which == 0 else 1 - core
+        for r in wanted:
             for c in range(col_blocks):
-                block = packed[position]
-                present = flags[r, c] > 0
                 rows, lanes = slice(r * edge, (r + 1) * edge), slice(c * edge, (c + 1) * edge)
-                w_buf[panel, half, rows, lanes] = jnp.where(present, block, jnp.zeros_like(block))
-                position = position + present.astype(jnp.int32)
-
-    dense(w_flags, same[home], pair, core)
-    dense(other_flags[home], other[home], pair, 1 - core)
+                w_buf[panel, half, rows, lanes] = packed[places[2 * o + which, r * col_blocks + c]]
+
+    every_row = range(row_blocks)
+    later_rows = range(1, row_blocks)
+    for packed in (*same, *other):
+        packed[blocks] = jnp.zeros((edge, edge), packed.dtype)
+    dense(home, 0, pair, every_row)
+    dense(home, 1, pair, every_row)
     total[...] = jnp.zeros_like(total)
 
     def forward(d, k):
@@ -603,37 +639,45 @@
 
             go_over(home - d, k).start()
 
-    def receive(d, k):
+    def flags_on(d):
         @pl.when(pair + d <= top)
         def _():
+            flags_arrival(home + d).wait_recv()
+
+            if d < top:
+                @pl.when(has_below)
+                def _():
+                    flags_go_down(d).start()
+
+        @pl.when(pair - d >= 0)
+        def _():
+            flags_arrival(home - d).wait_recv()
+
+            if d < top:
+                @pl.when(has_above)
+                def _():
+                    flags_go_up(d).start()
+
+    def middle(d, k):
+        @pl.when(pair + d < top)
+        def _():
             landed(home + d, k).wait_recv()
-            go_over(home + d, k).start()
-
-        @pl.when(pair - d >= 0)
-        def _():
-            landed(home - d, k).wait_recv()
-            go_over(home - d, k).start()
-
-    def middle(d):
-        @pl.when(pair + d < top)
-        def _():
-            landed(home + d, 1).wait_recv()
 
             @pl.when(has_below)
             def _():
-                go_down(d, 1).start()
-
-            go_over(home + d, 1).start()
+                go_down(d, k).start()
+
+            go_over(home + d, k).start()
 
         @pl.when(pair - d > 0)
         def _():
-            landed(home - d, 1).wait_recv()
+            landed(home - d, k).wait_recv()
 
             @pl.when(has_above)
             def _():
-                go_up(d, 1).start()
-
-            go_over(home - d, 1).start()
+                go_up(d, k).start()
+
+            go_over(home - d, k).start()
 
     def last(d):
         @pl.when(pair + d == top)
@@ -647,13 +691,14 @@
                 share(to_below, from_above)
                 shared_down().start()
 
-            landed(home + d, 1).wait_recv()
-
-            @pl.when(has_below)
-            def _():
-                go_down(d, 1).start()
-
-            go_over(home + d, 1).start()
+            for k in range(1, PIECES):
+                landed(home + d, k).wait_recv()
+
+                @pl.when(has_below)
+                def _(k=k):
+                    go_down(d, k).start()
+
+                go_over(home + d, k).start()
 
         @pl.when(pair - d == 0)
         def _():
@@ -666,28 +711,33 @@
                 share(to_above, from_below)
                 shared_up().start()
 
-            landed(home - d, 1).wait_recv()
-
-            @pl.when(has_above)
-            def _():
-                go_up(d, 1).start()
-
-            go_over(home - d, 1).start()
-
-    forward(1, FLAGS)
+            for k in range(1, PIECES):
+                landed(home - d, k).wait_recv()
+
+                @pl.when(has_above)
+                def _(k=k):
+                    go_up(d, k).start()
+
+                go_over(home - d, k).start()
+
+    def middles(d):
+        for k in range(1, PIECES):
+            middle(d, k)
+
     forward(1, 0)
-    h_put(beside, 0, 0, (beside, col)).wait_recv()
-    relay_across = h_put(beside, 0, 4, (across, col))
-    relay_across.start()
-    h_put(across, 1, 0, (beside, col)).wait_recv()
-    relay_beside = h_put(across, 1, 5, (beside, col))
-    relay_beside.start()
-    middle(1)
-    forward(2, FLAGS)
+    flags_on(1)
+    middles(1)
     last(1)
     forward(2, 0)
-    receive(3, FLAGS)
-    middle(2)
+    h_wait(beside, NEAR, 0)
+    relay_across = h_put(beside, 0, FAR, 2, (across, col))
+    relay_across.start()
+    h_wait(across, OVER, 1)
+    relay_beside = h_put(across, 1, FAR, 3, (beside, col))
+    relay_beside.start()
+    flags_on(2)
+    middles(2)
+    flags_on(3)
 
     totals[0] = jnp.where(pair > 0, own_both, 0)
     totals[1] = jnp.where(pair < top, own_both, 0)
@@ -698,8 +748,7 @@
 
             @pl.when((n >= 0) & (n <= top))
             def _(o=o, n=n, side=side):
-                crossed(o, FLAGS).wait_recv()
-                at_same, at_other = beyond(same_flags[o]), beyond(other_flags[o])
+                at_same, at_other = tabulate(o, 0), tabulate(o, 1)
                 start = starts[home, side]
                 starts[o, 0] = start + jnp.where(core == 0, 0, at_other)
                 starts[o, 1] = start + jnp.where(core == 0, at_same, 0)
@@ -725,29 +774,11 @@
             other[o][base + n] = source[within(starts[o, 1] + n, shared)]
 
     def spread(o, way_d):
-        dense(same_flags[o], same[o], pair + way_d, core)
-        dense(other_flags[o], other[o], pair + way_d, 1 - core)
-
-    h_put(beside, 1, 0, (beside, col)).wait_recv()
-    h_put(across, 0, 0, (beside, col)).wait_recv()
-    far = top
-
-    @pl.when(pair + far == top)
-    def _():
-        landed(home + far, 0).wait_recv()
-        go_over(home + far, 0).start()
-        shared_arrival(0).wait_recv()
-        shared_over(0).start()
-
-    @pl.when(pair - far == 0)
-    def _():
-        landed(home - far, 0).wait_recv()
-        go_over(home - far, 0).start()
-        shared_arrival(1).wait_recv()
-        shared_over(1).start()
-
-    h_put(opposite, 0, 0, (beside, col)).wait_recv()
-    h_put(opposite, 1, 0, (beside, col)).wait_recv()
+        dense(o, 0, pair + way_d, every_row)
+        dense(o, 1, pair + way_d, every_row)
+
+    h_wait(beside, NEAR, 1)
+    h_wait(across, OVER, 0)
     span = 2 * half_rows
     width = col_blocks * edge
 
@@ -756,72 +787,108 @@
         right = h_buf[panel].reshape(span, h_buf.shape[3])
         total[...] += contract(left, right)
 
-    def one_panel(step, carry):
-        add((pair + step) % panels)
-        return carry
-
-    add(pair)
-
-    @pl.when(pair + far == top)
-    def _():
-        shared_crossed(0).wait_recv()
-
-    @pl.when(pair - far == 0)
-    def _():
-        shared_crossed(1).wait_recv()
-
-    for side, way in ((0, 1), (1, -1)):
+    @pl.when(pair != opposite)
+    def _():
+        add(pair)
+
+    sides = ((0, 1), (1, -1))
+
+    def at_end(body):
+        for side, way in sides:
+            @pl.when(pair == (0, top)[side])
+            def _(side=side, way=way):
+                body(side, home + way * far, pair + way * far)
+
+    def far_first(side, o, panel):
+        landed(o, 0).wait_recv()
+        go_over(o, 0).start()
+        shared_arrival(side).wait_recv()
+        shared_over(side).start()
+        shared_crossed(side).wait_recv()
+
+    at_end(far_first)
+
+    for side, way in sides:
         for d in range(1, far):
             o, n = home + way * d, pair + way * d
 
             @pl.when((n >= 0) & (n <= top))
             def _(o=o, side=side, way=way, d=d):
-                for k in range(2):
+                for k in range(PIECES):
                     crossed(o, k).wait_recv()
                 fill(o, side)
                 spread(o, way * d)
 
+    def near(panel):
+        gap = panel - pair
+        return (gap < far) & (gap > -far)
+
     def near_panel(step, carry):
         panel = (pair + step) % panels
-        gap = panel - pair
-
-        @pl.when((gap < far) & (gap > -far))
+
+        @pl.when(near(panel) & (panel != opposite))
         def _():
             add(panel)
 
         return carry
 
+    def far_middle(side, o, panel):
+        for k in range(1, PIECES - 1):
+            landed(o, k).wait_recv()
+            go_over(o, k).start()
+
+    at_end(far_middle)
     lax.fori_loop(1, panels, near_panel, 0)
 
+    h_wait(opposite, FAR, 0)
+    h_wait(opposite, FAR, 1)
+
+    @pl.when(near(opposite))
+    def _():
+        add(opposite)
+
     is_end = (pair == 0) | (pair == top)
-    for side, way in ((0, 1), (1, -1)):
-        o = home + way * far
-
-        @pl.when(pair == (0, top)[side])
-        def _(o=o, side=side, way=way):
-            landed(o, 1).wait_recv()
-            go_over(o, 1).start()
-            crossed(o, 0).wait_recv()
-            fill(o, side)
-            dense(same_flags[o], same[o], pair + way * far, core)
+
+    def far_rows(side, o, panel):
+        for k in range(PIECES - 1):
+            crossed(o, k).wait_recv()
+        fill(o, side)
+        dense(o, 0, panel, range(1))
+        dense(o, 1, panel, range(1))
+
+    at_end(far_rows)
 
     @pl.when(is_end)
     def _():
         panel = top - pair
-        total[...] += contract(w_buf[panel, core], h_buf[panel, core])
-
-    for side, way in ((0, 1), (1, -1)):
-        o = home + way * far
-
-        @pl.when(pair == (0, top)[side])
-        def _(o=o, side=side, way=way):
-            crossed(o, 1).wait_recv()
-            dense(other_flags[o], other[o], pair + way * far, 1 - core)
+        left = w_buf[panel, :, :edge].reshape(2 * edge, width)
+        right = h_buf[panel, :, :edge].reshape(2 * edge, h_buf.shape[3])
+        total[...] += contract(left, right)
+
+    def far_same(side, o, panel):
+        landed(o, PIECES - 1).wait_recv()
+        go_over(o, PIECES - 1).start()
+        same[o][final_piece] = late_same[side ^ 1][...]
+        dense(o, 0, panel, later_rows)
+
+    at_end(far_same)
 
     @pl.when(is_end)
     def _():
         panel = top - pair
-        final = total[...] + contract(w_buf[panel, 1 - core], h_buf[panel, 1 - core])
+        total[...] += contract(w_buf[panel, core, edge:], h_buf[panel, core, edge:])
+
+    def far_other(side, o, panel):
+        crossed(o, PIECES - 1).wait_recv()
+        other[o][final_piece] = late_other[side ^ 1][...]
+        dense(o, 1, panel, later_rows)
+
+    at_end(far_other)
+
+    @pl.when(is_end)
+    def _():
+        panel = top - pair
+        final = total[...] + contract(w_buf[panel, 1 - core, edge:], h_buf[panel, 1 - core, edge:])
         out_ref[...] = final.astype(out_ref.dtype)
 
     @pl.when(jnp.logical_not(is_end))
@@ -832,9 +899,12 @@
     over_ref[0, 0] = line_over[2, 0] + line_over[3, 0]
     for n in range(2):
         agree(n, (beside, col)).wait_send()
-    for copy in h_copies + [relay_across, relay_beside]:
-        copy.wait_send()
-    go_over(home, FLAGS).wait_send()
+    both_halves = h_buf.at[row]
+    for number, device in ((0, (beside, col)), (1, (across, col))):
+        put(both_halves, both_halves, h_sent.at[number], h_landed.at[0, 0], device).wait_send()
+    relay_across.wait_send()
+    relay_beside.wait_send()
+    flags_cross(core).wait_send()
     go_over(home, WHOLE).wait_send()
 
     @pl.when(has_above)
@@ -850,47 +920,46 @@
     for d in range(far):
         @pl.when(has_below & (pair + d <= top))
         def _(d=d):
-            for k in range(3):
-                go_down(d, k).wait_send()
+            flags_go_down(d).wait_send()
+            all_pieces(home + d, down_sent.at[d]).wait_send()
 
         @pl.when(has_above & (pair - d >= 0))
         def _(d=d):
-            for k in range(3):
-                go_up(d, k).wait_send()
+            flags_go_up(d).wait_send()
+            all_pieces(home - d, up_sent.at[d]).wait_send()
 
     for d in range(1, panels):
         @pl.when(pair + d <= top)
         def _(d=d):
-            for k in range(3):
-                go_over(home + d, k).wait_send()
+            all_pieces(home + d, core_sent.at[mark(home + d)]).wait_send()
 
         @pl.when(pair - d >= 0)
         def _(d=d):
-            for k in range(3):
-                go_over(home - d, k).wait_send()
+            all_pieces(home - d, core_sent.at[mark(home - d)]).wait_send()
 
 
 def base_slots(blocks):
     return 2 * blocks // 3
 
 
-def early_slots(blocks):
-    return 2 * base_slots(blocks) // 3
+PIECES = 3
 
 
 def packed(weights, weight_flags, hamiltonian, ham_flags):
+    weights, weight_flags, hamiltonian, ham_flags = (
+        pltpu.with_memory_space_constraint(given, pltpu.HBM)
+        for given in (weights, weight_flags, hamiltonian, ham_flags.T)
+    )
     panels = lax.axis_size("row")
     half_rows, width = weights.shape
     panel_rows, slice_cols = hamiltonian.shape
     edge = half_rows // weight_flags.shape[0]
     blocks = weight_flags.size
-    shared = base_slots(blocks)
+    base = base_slots(blocks)
+    shared = base
     offsets = 2 * panels - 1
     dma = pltpu.SemaphoreType.DMA
-    hbm = pl.BlockSpec(memory_space=pl.ANY)
-
-    def many(shape, dtype, space):
-        return [space(shape, dtype) for _ in range(offsets)]
+    hbm = pl.BlockSpec(memory_space=pltpu.HBM)
 
     def slots(count):
         return pltpu.VMEM((count, edge, edge), jnp.bfloat16)
@@ -904,18 +973,19 @@
         in_specs=[hbm] * 4,
         out_specs=(pl.BlockSpec(memory_space=pltpu.VMEM), pl.BlockSpec(memory_space=pltpu.SMEM)),
         scratch_shapes=[
-            pltpu.SMEM(ham_flags.shape[::-1], ham_flags.dtype),
-            many(weight_flags.shape, weight_flags.dtype, pltpu.SMEM),
-            many(weight_flags.shape, weight_flags.dtype, pltpu.SMEM),
+            pltpu.SMEM(ham_flags.shape, ham_flags.dtype),
+            [pltpu.SMEM((2, *weight_flags.shape), weight_flags.dtype) for _ in range(offsets)],
+            pltpu.SMEM((2 * offsets, blocks), jnp.int32),
             pltpu.SMEM((blocks + 1,), jnp.int32),
-            pltpu.SMEM((offsets, 2), jnp.int32),
             pltpu.SMEM((offsets, 2), jnp.int32),
             pltpu.SMEM((2,), jnp.int32),
             pltpu.SMEM((4, 1), jnp.int32),
             slots(blocks),
             pltpu.VMEM(hamiltonian.shape, hamiltonian.dtype),
-            [slots(blocks) for _ in range(offsets)],
-            [slots(blocks) for _ in range(offsets)],
+            [slots(blocks + 1) for _ in range(offsets)],
+            [slots(blocks + 1) for _ in range(offsets)],
+            [slots(base // PIECES) for _ in range(2)],
+            [slots(base // PIECES) for _ in range(2)],
             slots(shared),
             slots(shared),
             slots(shared // 2),
@@ -923,22 +993,26 @@
             pltpu.VMEM((panels, 2, half_rows, width), jnp.bfloat16),
             pltpu.VMEM((panels, 2, panel_rows // 2, slice_cols), jnp.bfloat16),
             pltpu.VMEM((width, slice_cols), jnp.float32),
-            dma((3 + blocks,)),
-            dma((offsets, 3)),
-            dma((offsets, 3)),
-            dma((panels, 3)),
-            dma((panels, 3)),
-            dma((offsets, 3)),
+            dma((4,)),
+            dma((panels,)),
+            dma((panels - 1,)),
+            dma((panels - 1,)),
+            dma((1,)),
+            dma((panels - 1, PIECES)),
+            dma((panels, PIECES)),
+            dma((panels - 1,)),
+            dma((panels - 1,)),
+            dma((panels,)),
             dma((2, 2)),
             dma((2,)),
             dma((2,)),
-            dma((panels, 2)),
-            dma((6,)),
+            dma((3, 2)),
+            dma((4,)),
             dma((2,)),
             dma((2,)),
         ],
         compiler_params=pltpu.CompilerParams(collective_id=1, has_side_effects=True),
-    )(weight_flags, ham_flags.T, weights, hamiltonian)
+    )(weight_flags, ham_flags, weights, hamiltonian)
     return lax.cond(
         over[0, 0] > 0,
         lambda kept, *given: gathered(*given),

time: 43 us -> 40.4 us (0.940)
  local copies, waits for them, and re-layouts: 2.22 us -> 0.88 us
  Pallas kernels: 39.9 us -> 38.7 us
    unnamed x9 -> x1, local copies, waits for them, and re-layouts: 2.22 us -> 0.88 us
    pallas_call x1, Pallas kernels: 39.9 us -> 38.7 us  [packed(): pl.pallas_call(functools.partial(packed_kernel, panels), out_shape=(pltpu...]
where the time goes in v2:
time: 40.4 us; the launch traced here: 40.2 us
  Pallas kernels  38.7 us (96%)
  local copies, waits for them, and re-layouts  0.88 us (2%)
  between operations  0.65 us (2%)
    pallas_call x1, Pallas kernels, packed(): pl.pallas_call(functools.partial(packed_kernel, panels), out_shape=(pltpu...  38.7 us
    unnamed x1, local copies, waits for them, and re-layouts  0.88 us

profile of v2, /device:TPU:0, one launch (start us, length us, event | category | flops | bytes accessed | tf_op | source)
XLA Modules:
  0.0 40.2 jit_solution(1856221754034954074)
XLA Ops:
  0.0 38.7 %shard_map.48 = (bf16[768,512]{1,0:T(8,128)(2,1)S(1)}, s32[1,1]{1,0:T(1,128)}) custom-call(s32[3,6]{1,0:T(4,128)} %w_flags_hbm.1, s32[4,6]{1,0:T(4,128)} %bitcast.2, bf16[384,768]{1,0:T(8,128)(2,1)} %w_hbm.1, bf16[768,512]{1,0:T(8,128)(2,1)} %h_hbm.1), custom_call_target="tpu_custom_call" | custom-call | tf_op jit(solution)/shard_map/pallas_call | solution.py:967
  39.3 0.9 %copy.10 = bf16[768,512]{1,0:T(8,128)(2,1)} copy(bf16[768,512]{1,0:T(8,128)(2,1)S(1)} %get-tuple-element.25) | data formatting | bytes 1572864
  (1 shorter events, 0.0 us)

commit v3 on v2

--- a/solution.py
+++ b/solution.py
@@ -617,6 +617,17 @@
     dense(home, 0, pair, every_row)
     dense(home, 1, pair, every_row)
     total[...] = jnp.zeros_like(total)
+    span = 2 * half_rows
+    width = col_blocks * edge
+
+    def add(panel):
+        left = w_buf[panel].reshape(span, width)
+        right = h_buf[panel].reshape(span, h_buf.shape[3])
+        total[...] += contract(left, right)
+
+    @pl.when(pair == row)
+    def _():
+        add(pair)
 
     def forward(d, k):
         @pl.when(pair + d <= top)
@@ -763,9 +774,6 @@
 
     agree(0, (beside, col)).start()
     last(2)
-    agree(0, (beside, col)).wait_recv()
-    line_over[2, 0] = line_over[0, 0] + line_over[1, 0]
-    agree(1, (across, col)).start()
 
     def fill(o, side):
         source = (from_above, from_below)[side]
@@ -779,15 +787,7 @@
 
     h_wait(beside, NEAR, 1)
     h_wait(across, OVER, 0)
-    span = 2 * half_rows
-    width = col_blocks * edge
-
-    def add(panel):
-        left = w_buf[panel].reshape(span, width)
-        right = h_buf[panel].reshape(span, h_buf.shape[3])
-        total[...] += contract(left, right)
-
-    @pl.when(pair != opposite)
+    @pl.when((pair != row) & (pair != opposite))
     def _():
         add(pair)
 
@@ -807,6 +807,9 @@
         shared_crossed(side).wait_recv()
 
     at_end(far_first)
+    agree(0, (beside, col)).wait_recv()
+    line_over[2, 0] = line_over[0, 0] + line_over[1, 0]
+    agree(1, (across, col)).start()
 
     for side, way in sides:
         for d in range(1, far):
@@ -968,7 +971,7 @@
         functools.partial(packed_kernel, panels),
         out_shape=(
             pltpu.VMEM((width, slice_cols), jnp.bfloat16),
-            jax.ShapeDtypeStruct((1, 1), jnp.int32),
+            pltpu.SMEM((1, 1), jnp.int32),
         ),
         in_specs=[hbm] * 4,
         out_specs=(pl.BlockSpec(memory_space=pltpu.VMEM), pl.BlockSpec(memory_space=pltpu.SMEM)),

time: 40.4 us -> 38.3 us (0.948)
  Pallas kernels: 38.7 us -> 36.9 us
  between operations: 0.65 us -> 0.02 us
    pallas_call x1, Pallas kernels: 38.7 us -> 36.9 us  [packed(): pl.pallas_call(functools.partial(packed_kernel, panels), out_shape=(pltpu...]
where the time goes in v3:
time: 38.3 us; the launch traced here: 37.8 us
  Pallas kernels  36.9 us (96%)
  local copies, waits for them, and re-layouts  0.88 us (2%)
    pallas_call x1, Pallas kernels, packed(): pl.pallas_call(functools.partial(packed_kernel, panels), out_shape=(pltpu...  36.9 us
    unnamed x1, local copies, waits for them, and re-layouts  0.88 us

profile of v3, /device:TPU:0, one launch (start us, length us, event | category | flops | bytes accessed | tf_op | source)
XLA Modules:
  0.0 37.8 jit_solution(2100218394154468200)
XLA Ops:
  0.0 36.9 %shard_map.48 = (bf16[768,512]{1,0:T(8,128)(2,1)S(1)}, s32[1,1]{1,0:T(1,128)S(4)}) custom-call(s32[3,6]{1,0:T(4,128)} %w_flags_hbm.1, s32[4,6]{1,0:T(4,128)} %bitcast.2, bf16[384,768]{1,0:T(8,128)(2,1)} %w_hbm.1, bf16[768,512]{1,0:T(8,128)(2,1)} %h_hbm.1), custom_call_target="tpu_custom_call" | custom-call | tf_op jit(solution)/shard_map/pallas_call | solution.py:970
  37.0 0.9 %copy.10 = bf16[768,512]{1,0:T(8,128)(2,1)} copy(bf16[768,512]{1,0:T(8,128)(2,1)S(1)} %get-tuple-element.25) | data formatting | bytes 1572864
  (1 shorter events, 0.0 us)

commit v4 on v3

--- a/solution.py
+++ b/solution.py
@@ -383,7 +383,8 @@
     part = shared // 2
     base = base_slots(blocks)
     rest = blocks - base
-    slices = [slice(base * k // PIECES, base * (k + 1) // PIECES) for k in range(PIECES)]
+    cuts = piece_cuts(base)
+    slices = [slice(*cuts[k:k + 2]) for k in range(PIECES)]
     final_piece = slices[-1]
     WHOLE = 0
     far = top
@@ -948,6 +949,10 @@
 PIECES = 3
 
 
+def piece_cuts(base):
+    return (0, base // 3, 7 * base // 12, base)
+
+
 def packed(weights, weight_flags, hamiltonian, ham_flags):
     weights, weight_flags, hamiltonian, ham_flags = (
         pltpu.with_memory_space_constraint(given, pltpu.HBM)
@@ -960,6 +965,7 @@
     blocks = weight_flags.size
     base = base_slots(blocks)
     shared = base
+    cuts = piece_cuts(base)
     offsets = 2 * panels - 1
     dma = pltpu.SemaphoreType.DMA
     hbm = pl.BlockSpec(memory_space=pltpu.HBM)
@@ -987,8 +993,8 @@
             pltpu.VMEM(hamiltonian.shape, hamiltonian.dtype),
             [slots(blocks + 1) for _ in range(offsets)],
             [slots(blocks + 1) for _ in range(offsets)],
-            [slots(base // PIECES) for _ in range(2)],
-            [slots(base // PIECES) for _ in range(2)],
+            [slots(cuts[-1] - cuts[-2]) for _ in range(2)],
+            [slots(cuts[-1] - cuts[-2]) for _ in range(2)],
             slots(shared),
             slots(shared),
             slots(shared // 2),

time: 38.3 us -> 38 us (level)
  Pallas kernels: 36.9 us -> 36.5 us
where the time goes in v4:
time: 38 us; the launch traced here: 37.5 us
  Pallas kernels  36.5 us (96%)
  local copies, waits for them, and re-layouts  0.88 us (2%)
    pallas_call x1, Pallas kernels, packed(): pl.pallas_call(functools.partial(packed_kernel, panels), out_shape=(pltpu...  36.5 us
    unnamed x1, local copies, waits for them, and re-layouts  0.88 us

profile of v4, /device:TPU:0, one launch (start us, length us, event | category | flops | bytes accessed | tf_op | source)
XLA Modules:
  0.0 37.5 jit_solution(8234462818034373609)
XLA Ops:
  0.0 36.5 %shard_map.48 = (bf16[768,512]{1,0:T(8,128)(2,1)S(1)}, s32[1,1]{1,0:T(1,128)S(4)}) custom-call(s32[3,6]{1,0:T(4,128)} %w_flags_hbm.1, s32[4,6]{1,0:T(4,128)} %bitcast.2, bf16[384,768]{1,0:T(8,128)(2,1)} %w_hbm.1, bf16[768,512]{1,0:T(8,128)(2,1)} %h_hbm.1), custom_call_target="tpu_custom_call" | custom-call | tf_op jit(solution)/shard_map/pallas_call | solution.py:976
  36.6 0.9 %copy.10 = bf16[768,512]{1,0:T(8,128)(2,1)} copy(bf16[768,512]{1,0:T(8,128)(2,1)S(1)} %get-tuple-element.25) | data formatting | bytes 1572864
  (1 shorter events, 0.0 us)

commit v5 on v4

--- a/solution.py
+++ b/solution.py
@@ -828,7 +828,7 @@
         return (gap < far) & (gap > -far)
 
     def near_panel(step, carry):
-        panel = (pair + step) % panels
+        panel = (pair + jnp.where(pair == top, panels - step, step)) % panels
 
         @pl.when(near(panel) & (panel != opposite))
         def _():
@@ -841,8 +841,9 @@
             landed(o, k).wait_recv()
             go_over(o, k).start()
 
+    lax.fori_loop(1, 2, near_panel, 0)
     at_end(far_middle)
-    lax.fori_loop(1, panels, near_panel, 0)
+    lax.fori_loop(2, panels, near_panel, 0)
 
     h_wait(opposite, FAR, 0)
     h_wait(opposite, FAR, 1)

time: 38 us -> 38 us (level)
  no operation moved by 1% of the time
where the time goes in v5:
time: 38 us; the launch traced here: 37.5 us
  Pallas kernels  36.5 us (96%)
  local copies, waits for them, and re-layouts  0.88 us (2%)
    pallas_call x1, Pallas kernels, packed(): pl.pallas_call(functools.partial(packed_kernel, panels), out_shape=(pltpu...  36.5 us
    unnamed x1, local copies, waits for them, and re-layouts  0.88 us

profile of v5, /device:TPU:0, one launch (start us, length us, event | category | flops | bytes accessed | tf_op | source)
XLA Modules:
  0.0 37.5 jit_solution(10697684374426157394)
XLA Ops:
  0.0 36.5 %shard_map.48 = (bf16[768,512]{1,0:T(8,128)(2,1)S(1)}, s32[1,1]{1,0:T(1,128)S(4)}) custom-call(s32[3,6]{1,0:T(4,128)} %w_flags_hbm.1, s32[4,6]{1,0:T(4,128)} %bitcast.2, bf16[384,768]{1,0:T(8,128)(2,1)} %w_hbm.1, bf16[768,512]{1,0:T(8,128)(2,1)} %h_hbm.1), custom_call_target="tpu_custom_call" | custom-call | tf_op jit(solution)/shard_map/pallas_call | solution.py:977
  36.6 0.9 %copy.10 = bf16[768,512]{1,0:T(8,128)(2,1)} copy(bf16[768,512]{1,0:T(8,128)(2,1)S(1)} %get-tuple-element.25) | data formatting | bytes 1572864
  (1 shorter events, 0.0 us)
